TPU v7x, 256 devices: a whole 4x4x8 slice. The times are simulated.
256 devices in a mesh: tm: 32 (over y_lo, z, core), gy: 8 (over y_hi, x).
Axes of the slice: x: 4, y: 4 (y_hi: 2, y_lo: 2; y = y_hi * 2 + y_lo), z: 8, core: 2. Of those that a mesh axis runs over, the one named last changes fastest.
Arguments:
- magnetic: bfloat16 [32, 3, 3, 1024, 1024], P('tm', None, None, 'gy'), may hold values from -6 to 6
- velocity: bfloat16 [32, 3, 1, 1024, 1024], P('tm', None, None, 'gy'), may hold values from -6 to 6
- mode_bin: int32 [1024, 1024], P(None, 'gy'), may hold values from 0 to 127, as said below
- omega_edges: int32 [9], replicated, may hold values from 0 to 32, as said below
Outputs:
- power: float32 [32, 1024, 1024], P('tm', None, 'gy')
- spectrum: float32 [8, 128], replicated
Inputs may be any that keep to these rules, and one draw needn't show every extreme that they name: mode_bin = 16 * p + q, where p is a level of min(kz, 1024 - kz) and q a level of min(ky, 1024 - ky); levels never fall as the wavenumber rises, and every value occurs. `omega_edges`: edges rise strictly, the first 0 and the last 32.
All inputs are finite; a program needn't handle non-finite values.
Results may differ from a plain program's by a relative error of at most 0.004.
The roundings to bfloat16 on the way count: a program that leaves them out, or rounds other values in their place, can miss the bound.
Values may be sent and summed in bfloat16 or wider, within the bound.
No kernel may reach another device: no remote copies, remote signals or barrier semaphores. Data moves between devices by JAX's collectives and lax.ppermute only.
A program may use at most 128 MiB of HBM per device.

v0:
```python
import math

import jax
import jax.numpy as jnp
from jax import lax
from jax.sharding import PartitionSpec as P

NBP = 8
NBQ = 16
NB_W = 8


hall_coef = 1.0
highest = lax.Precision.HIGHEST


def extended(cells, sides, width):
    for axis, dim in sides:
        count = lax.axis_size(axis)
        head = lax.slice_in_dim(cells, 0, width, axis=dim)
        tail = lax.slice_in_dim(cells, cells.shape[dim] - width, cells.shape[dim], axis=dim)
        cells = jnp.concatenate(
            [
                lax.ppermute(tail, axis, [(i, (i + 1) % count) for i in range(count)]),
                cells,
                lax.ppermute(head, axis, [((i + 1) % count, i) for i in range(count)]),
            ],
            axis=dim,
        )
    return cells


def window_taper_for(sample_moments, every_time_sample):
    return 0.5 - 0.5 * jnp.cos(
        2.0 * math.pi * (sample_moments.astype(jnp.float32) + 0.5) / every_time_sample
    )


def temporal_coefficients(angular_frequency, sample_moments, every_time_sample):
    phase_angles = jnp.mod(
        angular_frequency[:, None] * sample_moments[None, :], every_time_sample
    ).astype(jnp.float32)
    angles = 2.0 * math.pi * phase_angles / every_time_sample
    taper_weight = window_taper_for(sample_moments, every_time_sample)[None, :]
    return (
        (taper_weight * jnp.cos(angles)).astype(jnp.bfloat16),
        (-taper_weight * jnp.sin(angles)).astype(jnp.bfloat16),
    )


def dft_tables(length):
    series = jnp.arange(length, dtype=jnp.int32)
    phase_angles = jnp.mod(series[:, None] * series[None, :], length).astype(jnp.float32)
    angles = 2.0 * math.pi * phase_angles / length
    return (jnp.cos(angles).astype(jnp.bfloat16), jnp.sin(angles).astype(jnp.bfloat16))


def z_slope(values):
    return (jnp.roll(values, -1, axis=-1) - jnp.roll(values, 1, axis=-1)) * 0.5


def z_turn(re_part, im_part):
    zcos_tab, zsin_tab = dft_tables(re_part.shape[-1])
    turned_re = jnp.dot(re_part, zcos_tab, preferred_element_type=jnp.float32) + jnp.dot(
        im_part, zsin_tab, preferred_element_type=jnp.float32
    )
    turned_im = jnp.dot(im_part, zcos_tab, preferred_element_type=jnp.float32) - jnp.dot(
        re_part, zsin_tab, preferred_element_type=jnp.float32
    )
    return jnp.stack([turned_re, turned_im]).astype(jnp.bfloat16)


def electric_of(magnetic, velocity, slope_magz, slope_magx):
    inner = magnetic[:, :, 1:-1].astype(jnp.float32)
    x_slope = (
        magnetic[:, :, 2:].astype(jnp.float32) - magnetic[:, :, :-2].astype(jnp.float32)
    ) * 0.5
    mag_x, mag_y, mag_z = (inner[:, 0], inner[:, 1], inner[:, 2])
    cur_x = slope_magz - z_slope(mag_y)
    cur_y = z_slope(mag_x) - x_slope[:, 2]
    cur_z = x_slope[:, 1] - slope_magx
    flow = velocity.astype(jnp.float32)
    vel_x, vel_y, vel_z = (flow[:, 0], flow[:, 1], flow[:, 2])
    elec_x = -(vel_y * mag_z - vel_z * mag_y) + hall_coef * (cur_y * mag_z - cur_z * mag_y)
    elec_y = -(vel_z * mag_x - vel_x * mag_z) + hall_coef * (cur_z * mag_x - cur_x * mag_z)
    elec_z = -(vel_x * mag_y - vel_y * mag_x) + hall_coef * (cur_x * mag_y - cur_y * mag_x)
    return jnp.stack([elec_x, elec_y, elec_z], axis=1)


def body(magnetic, velocity, mode_bin, omega_edges):
    face_rows = jnp.stack([magnetic[:, 2, 1:-1], magnetic[:, 0, 1:-1]], axis=1)
    padded = extended(face_rows, (("gy", 3),), 1)
    slopes = (
        padded[:, :, :, 2:].astype(jnp.float32) - padded[:, :, :, :-2].astype(jnp.float32)
    ) * 0.5
    electric = electric_of(magnetic, velocity, slopes[:, 0], slopes[:, 1]).astype(jnp.bfloat16)
    local_t = electric.shape[0]
    z_count = electric.shape[-1]
    every_time_sample = local_t * lax.axis_size("tm")
    half_count = every_time_sample // 2
    owner_rank = lax.axis_index("tm")
    angular_frequency = owner_rank * local_t + jnp.arange(local_t, dtype=jnp.int32) - half_count
    time_segment = lax.all_gather(electric, "tm", axis=0, tiled=True)
    sample_moments = jnp.arange(time_segment.shape[0], dtype=jnp.int32)
    coefficient_real, coefficient_imaginary = temporal_coefficients(
        angular_frequency, sample_moments, every_time_sample
    )
    re_part = jnp.einsum(
        "wt,tcxyz->wcxyz", coefficient_real, time_segment, preferred_element_type=jnp.float32
    )
    im_part = jnp.einsum(
        "wt,tcxyz->wcxyz", coefficient_imaginary, time_segment, preferred_element_type=jnp.float32
    )
    moved = lax.all_to_all(
        z_turn(re_part.astype(jnp.bfloat16), im_part.astype(jnp.bfloat16)),
        "gy",
        split_axis=5,
        concat_axis=4,
        tiled=True,
    )
    y_count = moved.shape[4]
    ycos_tab, ysin_tab = dft_tables(y_count)
    wave_re = jnp.einsum(
        "wcxyk,yq->wcxqk", moved[0], ycos_tab, preferred_element_type=jnp.float32
    ) + jnp.einsum("wcxyk,yq->wcxqk", moved[1], ysin_tab, preferred_element_type=jnp.float32)
    wave_im = jnp.einsum(
        "wcxyk,yq->wcxqk", moved[1], ycos_tab, preferred_element_type=jnp.float32
    ) - jnp.einsum("wcxyk,yq->wcxqk", moved[0], ysin_tab, preferred_element_type=jnp.float32)
    power_map = jnp.sum(wave_re * wave_re + wave_im * wave_im, axis=(1, 2)) / (
        every_time_sample * y_count * z_count
    )
    kz_local = power_map.shape[2]
    block_rows = min(64, y_count)
    bin_total = NBP * NBQ
    bin_range = jnp.arange(bin_total, dtype=jnp.int32)

    def add_block(step_num, summed):
        row_block = lax.dynamic_slice_in_dim(
            power_map, step_num * block_rows, block_rows, 1
        ).reshape(local_t, block_rows * kz_local)
        bin_ids = lax.dynamic_slice_in_dim(mode_bin, step_num * block_rows, block_rows, 0).reshape(
            block_rows * kz_local
        )
        onehot = (bin_ids[:, None] == bin_range[None, :]).astype(jnp.float32)
        return summed + jnp.dot(row_block, onehot, precision=highest)

    by_mode = lax.fori_loop(
        0, y_count // block_rows, add_block, jnp.zeros((local_t, bin_total), jnp.float32)
    )
    omega = owner_rank * local_t + jnp.arange(local_t, dtype=jnp.int32)
    member = (
        (omega[None, :] >= omega_edges[:-1, None]) & (omega[None, :] < omega_edges[1:, None])
    ).astype(jnp.float32)
    partial_value = jnp.dot(member, by_mode, precision=highest)
    binned = lax.psum(partial_value, ("tm", "gy"))
    spectrum = jnp.log(
        binned * (NB_W * bin_total) / (every_time_sample * y_count * z_count) + 1e-06
    )
    return (power_map, spectrum)


def solution(mesh):
    return jax.shard_map(
        body,
        mesh=mesh,
        in_specs=(
            P("tm", None, None, "gy", None),
            P("tm", None, None, "gy", None),
            P(None, "gy"),
            P(),
        ),
        out_specs=(P("tm", None, "gy"), P()),
        check_vma=False,
    )
```

profile of v0, /device:TPU:1, one launch (start us, length us, event | category | flops | bytes accessed | tf_op | source)
XLA Modules:
  0.0 512.5 jit_solution(18000967554781323091)
XLA Ops:
  8.5 6.0 %collective-permute-start = (bf16[1,2,1,1,1024]{4,3,2,1,0:T(2,128)(2,1)S(1)}, bf16[1,2,1,1,1024]{4,3,2,1,0:T(2,128)(2,1)S(1)}, u32[]{:S(2)}, u32[]{:S(2)}) collective-permute-start(bf16[1,2,1,1,1024]{4,3,2,1,0:T(2,128)(2,1)S(1)} %get-tuple-element.139), channel_id=1, source_target_pairs={{1,0},{2,1},{3,2},{4,3},{5,4},{6,5},{7,6},{0,7},{9,8},{10,9},{11,1... | collective-permute-start | bytes 12296 | tf_op jit(solution)/shard_map/ppermute | solution.py:26
  16.7 3.9 collective-permute-done.1
  23.7 142.3 %all-gather.2.cloned.1.call-done = bf16[32,3,1,128,1024]{4,3,2,1,0:T(8,128)(2,1)} async-done(((bf16[1,3,1,128,1024]{4,3,2,1,0:T(8,128)(2,1)}), bf16[32,3,1,128,1024]{4,3,2,1,0:T(8,128)(2,1)}) %all-gather.2.cloned.1.call-update) | async-done | bytes 25165840 | tf_op jit(solution)/shard_map/all_gather | solution.py:103
  166.0 24.4 %fusion.5 = bf16[1,3,128,1024]{3,0,2,1:T(2,128)(2,1)S(1)} fusion(bf16[32,3,128,1024]{3,2,1,0:T(8,128)(2,1)} %bitcast.97, s32[]{:T(128)S(6)} %sub.139), kind=kOutput, calls=%fused_computation.8 | convolution fusion | flops 25166528 | bytes 25952260 | tf_op jit(solution)/shard_map/wt,tcxyz->wcxyz/dot_general | solution.py:111
  190.5 24.9 %fusion.7 = bf16[1,3,128,1024]{3,0,2,1:T(2,128)(2,1)S(1)} fusion(bf16[32,3,128,1024]{3,2,1,0:T(8,128)(2,1)} %bitcast.98, s32[]{:T(128)S(6)} %sub.139), kind=kOutput, calls=%fused_computation.10 | convolution fusion | flops 25166496 | bytes 25952260 | tf_op jit(solution)/shard_map/wt,tcxyz->wcxyz/dot_general | solution.py:108
  215.4 16.1 %fusion.21 = f32[3,128,1024]{2,1,0:T(8,128)S(1)} fusion(bf16[1,3,128,1024]{3,0,2,1:T(2,128)(2,1)S(1)} %fusion.7), kind=kOutput, calls=%fused_computation.27 | convolution fusion | flops 821035008 | bytes 2359296 | tf_op jit(solution)/shard_map/dot_general | solution.py:67
  231.5 16.1 %fusion.23 = f32[3,128,1024]{2,1,0:T(8,128)S(1)} fusion(bf16[1,3,128,1024]{3,0,2,1:T(2,128)(2,1)S(1)} %fusion.5), kind=kOutput, calls=%fused_computation.28 | convolution fusion | flops 821035008 | bytes 2359296 | tf_op jit(solution)/shard_map/dot_general | solution.py:64
  247.6 16.5 %fusion.42 = bf16[1,1,3,1,128,1024]{5,4,2,3,1,0:T(8,128)(2,1)S(1)} fusion(f32[3,128,1024]{2,1,0:T(8,128)S(1)} %fusion.21, bf16[1,3,128,1024]{3,0,2,1:T(2,128)(2,1)S(1)} %fusion.5), kind=kOutput, calls=%fused_computation.41 | convolution fusion | flops 821821440 | bytes 3145728 | tf_op jit(solution)/shard_map/dot_general | solution.py:67
  264.1 16.3 %fusion.39 = bf16[1,1,3,1,128,1024]{5,4,2,3,1,0:T(8,128)(2,1)S(1)} fusion(f32[3,128,1024]{2,1,0:T(8,128)S(1)} %fusion.23, bf16[1,3,128,1024]{3,0,2,1:T(2,128)(2,1)S(1)} %fusion.7), kind=kOutput, calls=%fused_computation.40 | convolution fusion | flops 821821440 | bytes 3145728 | tf_op jit(solution)/shard_map/dot_general | solution.py:64
  280.6 3.0 copy.44
  283.6 6.7 %all-to-all-start = ((bf16[2,1,3,1,128,1024]{4,0,3,2,1,5:T(2,128)(2,1)}), bf16[2,1,3,1,128,1024]{4,0,3,2,1,5:T(2,128)(2,1)S(1)}, u32[]{:S(2)}, u32[]{:S(2)}) async-start(bf16[2,1,3,1,128,1024]{4,0,3,2,1,5:T(2,128)(2,1)} %copy.44), calls=%async_computation | async-start | bytes 3145728 | tf_op jit(solution)/shard_map/all_to_all | solution.py:114
  290.4 22.9 %all-to-all-done = bf16[2,1,3,1,128,1024]{4,0,3,2,1,5:T(2,128)(2,1)S(1)} async-done(((bf16[2,1,3,1,128,1024]{4,0,3,2,1,5:T(2,128)(2,1)}), bf16[2,1,3,1,128,1024]{4,0,3,2,1,5:T(2,128)(2,1)S(1)}, u32[]{:S(2)}, u32[]{:S(2)}) %all-to-all-start) | async-done | bytes 1572896 | tf_op jit(solution)/shard_map/all_to_all | solution.py:114
  313.3 2.4 copy.45
  315.8 17.9 %fusion.29 = f32[1024,3,128]{2,0,1:T(8,128)S(1)} fusion(bf16[3,1024,128]{2,1,0:T(8,128)(2,1)S(1)} %bitcast.104), kind=kOutput, calls=%fused_computation.31 | convolution fusion | flops 821035008 | bytes 2359296 | tf_op jit(solution)/shard_map/wcxyk,yq->wcxqk/dot_general | solution.py:126
  333.7 18.0 %fusion.19 = f32[1024,3,128]{2,0,1:T(8,128)S(1)} fusion(bf16[3,1024,128]{2,1,0:T(8,128)(2,1)S(1)} %bitcast.105), kind=kOutput, calls=%fused_computation.26 | convolution fusion | flops 821035008 | bytes 2359296 | tf_op jit(solution)/shard_map/wcxyk,yq->wcxqk/dot_general | solution.py:125
  351.6 18.0 %fusion.17 = f32[1024,3,128]{2,0,1:T(8,128)S(1)} fusion(bf16[3,1024,128]{2,1,0:T(8,128)(2,1)S(1)} %bitcast.102), kind=kOutput, calls=%fused_computation.25 | convolution fusion | flops 821035008 | bytes 2359296 | tf_op jit(solution)/shard_map/wcxyk,yq->wcxqk/dot_general | solution.py:128
  369.6 18.0 %add_reduce_fusion = f32[1024,128]{1,0:T(8,128)S(1)} fusion(f32[1024,3,128]{2,0,1:T(8,128)S(1)} %fusion.29, f32[1024,3,128]{2,0,1:T(8,128)S(1)} %fusion.17, f32[1024,3,128]{2,0,1:T(8,128)S(1)} %fusion.19, bf16[3,1024,128]{2,1,0:T(8,128)(2,1)S(1)} %bitcast.103), kind=kOutput, calls=%fused_computation.36 | convolution fusion | flops 823263232 | bytes 6029312 | tf_op jit(solution)/shard_map/wcxyk,yq->wcxqk/dot_general | solution.py:123
  387.7 41.5 %while.14 = (s32[]{:T(128)}, f32[1,128]{1,0:T(1,128)S(1)}, f32[1,1024,128]{2,1,0:T(8,128)S(1)}, s32[1024,128]{1,0:T(8,128)}, s32[]{:T(128)}, /*index=5*/s32[]{:T(128)}, s32[]{:T(128)}, s32[]{:T(128)}) while((s32[]{:T(128)}, f32[1,128]{1,0:T(1,128)S(1)}, f32[1,1024,128]{2,1,0:T(8,128)S(1)}, s32[1024,128]{1,0:T(8,128)}, s32[]{:T(128)}, ...), condition=%wide.region_2.3_spmd.clone, body=%wide.region_1.2_spmd.clone.sunk | while | flops 13631751 | bytes 197789 | solution.py:147
  388.5 1.8 fusion.113
  393.7 1.8 fusion.113
  396.3 1.8 fusion.113
  398.9 1.8 fusion.113
  401.5 1.8 fusion.113
  404.1 1.8 fusion.113
  406.6 1.8 fusion.113
  409.2 1.8 fusion.113
  414.4 1.8 fusion.113
  417.0 1.8 fusion.113
  422.2 1.8 fusion.113
  424.8 1.8 fusion.113
  427.4 1.8 fusion.113
  429.3 75.6 %psum.7 = f32[8,128]{1,0:T(8,128)S(1)} all-reduce(f32[8,128]{1,0:T(8,128)S(1)} %broadcast_multiply_fusion), channel_id=1, replica_groups=mesh['tm'=32,'gy'=8] {'tm','gy'}, use_global_device_ids=true, to_apply=%region_3.4 | all-reduce | flops 1024 | bytes 8192 | tf_op jit(solution)/shard_map/psum | solution.py:155
  (69 shorter events, 25.3 us)
Async XLA Ops:
  7.2 8.7 %copy-start = (bf16[1,3,3,128,1024]{4,3,2,1,0:T(8,128)(2,1)S(1)}, bf16[1,3,3,128,1024]{4,3,2,1,0:T(8,128)(2,1)}, u32[]{:S(2)}) copy-start(bf16[1,3,3,128,1024]{4,3,2,1,0:T(8,128)(2,1)} %param.6) | copy-start | bytes 7077892
  7.2 158.9 %all-gather.2.cloned.1.call-start = ((), (), s32[]{:S(2)}) async-start(), calls=%async_computation.1 | async-start | bytes 25952256 | tf_op jit(solution)/shard_map/all_gather | solution.py:103
  8.5 8.2 %collective-permute-start = (bf16[1,2,1,1,1024]{4,3,2,1,0:T(2,128)(2,1)S(1)}, bf16[1,2,1,1,1024]{4,3,2,1,0:T(2,128)(2,1)S(1)}, u32[]{:S(2)}, u32[]{:S(2)}) collective-permute-start(bf16[1,2,1,1,1024]{4,3,2,1,0:T(2,128)(2,1)S(1)} %get-tuple-element.139), channel_id=1, source_target_pairs={{1,0},{2,1},{3,2},{4,3},{5,4},{6,5},{7,6},{0,7},{9,8},{10,9},{11,1... | collective-permute-start | bytes 12296 | tf_op jit(solution)/shard_map/ppermute | solution.py:26
  14.5 2.0 copy-start.2
  14.5 6.1 %collective-permute-start.1 = (bf16[1,2,1,1,1024]{4,3,2,1,0:T(2,128)(2,1)S(1)}, bf16[1,2,1,1,1024]{4,3,2,1,0:T(2,128)(2,1)S(1)}, u32[]{:S(2)}, u32[]{:S(2)}) collective-permute-start(bf16[1,2,1,1,1024]{4,3,2,1,0:T(2,128)(2,1)S(1)} %get-tuple-element.140), channel_id=1, source_target_pairs={{0,1},{1,2},{2,3},{3,4},{4,5},{5,6},{6,7},{7,0},{8,9},{9,10},{10,1... | collective-permute-start | bytes 12296 | tf_op jit(solution)/shard_map/ppermute | solution.py:24
  280.4 9.9 %copy-start.3 = (s32[9]{0:T(128)S(1)}, s32[9]{0:T(128)}, u32[]{:S(2)}) copy-start(s32[9]{0:T(128)} %param.9) | copy-start | bytes 112
  283.6 29.7 %all-to-all-start = ((bf16[2,1,3,1,128,1024]{4,0,3,2,1,5:T(2,128)(2,1)}), bf16[2,1,3,1,128,1024]{4,0,3,2,1,5:T(2,128)(2,1)S(1)}, u32[]{:S(2)}, u32[]{:S(2)}) async-start(bf16[2,1,3,1,128,1024]{4,0,3,2,1,5:T(2,128)(2,1)} %copy.44), calls=%async_computation | async-start | bytes 3145728 | tf_op jit(solution)/shard_map/all_to_all | solution.py:114
  429.2 76.3 %copy-start.1 = (f32[1,1024,128]{2,1,0:T(8,128)}, f32[1,1024,128]{2,1,0:T(8,128)S(1)}, u32[]{:S(2)}) copy-start(f32[1,1024,128]{2,1,0:T(8,128)S(1)} %get-tuple-element.195) | copy-start | bytes 1572868
Sparse Core Ops, SparseCore 0:
  23.8 142.1 all-gather.1
where the time goes:
time: 518 us; the launch traced here: 513 us
  matrix products  215 us (42%)
  waiting for transfers between devices  169 us (33%)
  blocking collectives  75.6 us (15%)
  local copies, waits for them, and re-layouts  19.7 us (4%)
  between operations  14.5 us (3%)
  starting transfers between devices  12.7 us (2%)
  other arithmetic  5.55 us (1%)
    all_gather x1, waiting for transfers between devices, body(): time_segment = lax.all_gather(electric, 'tm', axis=0, tiled=True)  142 us
    psum x1, blocking collectives, body(): binned = lax.psum(partial_value, ('tm', 'gy'))  75.6 us
    dot_general x16, matrix products, add_block(): return summed + jnp.dot(row_block, onehot, precision=highest)  28.7 us
    dot_general x1, matrix products, body(): jnp.einsum('wt,tcxyz->wcxyz', coefficient_real, time_segment, preferred_e...  24.9 us
    dot_general x1, matrix products, body(): jnp.einsum('wt,tcxyz->wcxyz', coefficient_imaginary, time_segment, prefer...  24.4 us
    all_to_all x1, waiting for transfers between devices, body(): lax.all_to_all(z_turn(re_part.astype(jnp.bfloat16), im_part.astype(jnp.bf...  22.9 us
    dot_general x1, matrix products, body(): jnp.einsum('wcxyk,yq->wcxqk', moved[0], ycos_tab, preferred_element_type=...  18 us
    dot_general x1, matrix products, body(): jnp.einsum('wcxyk,yq->wcxqk', moved[1], ysin_tab, preferred_element_type=...  18 us
  transfers between devices with their start and end apart: 4, of which 3 were waited for; matrix products, arithmetic and copies ran while one was open for 0% of the time, Pallas kernels for 0%

commit v1 on v0

v1 whole, which is shorter than its diff:
```python
import math

import jax
import jax.numpy as jnp
import numpy as np
from jax import lax
from jax.experimental import pallas as pl
from jax.experimental.pallas import tpu as pltpu
from jax.sharding import PartitionSpec as P

NBP = 8
NBQ = 16
NB_W = 8
BINS = NBP * NBQ
N = 1024
NT = 32
SLAB = 128
HALF = NT // 2
f32 = jnp.float32
bf16 = jnp.bfloat16
VMEM = pl.BlockSpec(memory_space=pltpu.VMEM)


def electric_kernel(mag_ref, vel_ref, low_ref, high_ref, out_ref, bx_ref, bz_ref):
    bx_ref[0:8, :] = jnp.broadcast_to(low_ref[0:1, :].astype(f32), (8, N))
    bz_ref[0:8, :] = jnp.broadcast_to(low_ref[1:2, :].astype(f32), (8, N))
    bx_ref[SLAB + 8 : SLAB + 16, :] = jnp.broadcast_to(high_ref[0:1, :].astype(f32), (8, N))
    bz_ref[SLAB + 8 : SLAB + 16, :] = jnp.broadcast_to(high_ref[1:2, :].astype(f32), (8, N))

    def widen(group, carry):
        rows = pl.ds(pl.multiple_of(group * 8, 8), 8)
        inside = pl.ds(pl.multiple_of(group * 8 + 8, 8), 8)
        bx_ref[inside, :] = mag_ref[0, 0, 1, rows, :].astype(f32)
        bz_ref[inside, :] = mag_ref[0, 2, 1, rows, :].astype(f32)
        return carry

    lax.fori_loop(0, SLAB // 8, widen, 0)
    row = lax.broadcasted_iota(jnp.int32, (8, N), 0)
    half_row = lax.broadcasted_iota(jnp.int32, (8, 128), 0)

    def y_slope(ref, group):
        before = ref[pl.ds(pl.multiple_of(group * 8, 8), 8), :]
        here = ref[pl.ds(pl.multiple_of(group * 8 + 8, 8), 8), :]
        after = ref[pl.ds(pl.multiple_of(group * 8 + 16, 8), 8), :]
        up = jnp.where(row == 7, pltpu.roll(after, 7, 0), pltpu.roll(here, 7, 0))
        down = jnp.where(row == 0, pltpu.roll(before, 1, 0), pltpu.roll(here, 1, 0))
        return here, (up - down) * 0.5

    def z_slope(v):
        return (pltpu.roll(v, N - 1, 1) - pltpu.roll(v, 1, 1)) * 0.5

    def step(group, carry):
        rows = pl.ds(pl.multiple_of(group * 8, 8), 8)

        def x_slope(c):
            return (mag_ref[0, c, 2, rows, :].astype(f32) - mag_ref[0, c, 0, rows, :].astype(f32)) * 0.5

        mag_x, slope_x = y_slope(bx_ref, group)
        mag_z, slope_z = y_slope(bz_ref, group)
        mag_y = mag_ref[0, 1, 1, rows, :].astype(f32)
        cur_x = slope_z - z_slope(mag_y)
        cur_y = z_slope(mag_x) - x_slope(2)
        cur_z = x_slope(1) - slope_x
        vel_x = vel_ref[0, 0, 0, rows, :].astype(f32)
        vel_y = vel_ref[0, 1, 0, rows, :].astype(f32)
        vel_z = vel_ref[0, 2, 0, rows, :].astype(f32)
        field = (
            -(vel_y * mag_z - vel_z * mag_y) + (cur_y * mag_z - cur_z * mag_y),
            -(vel_z * mag_x - vel_x * mag_z) + (cur_z * mag_x - cur_x * mag_z),
            -(vel_x * mag_y - vel_y * mag_x) + (cur_x * mag_y - cur_y * mag_x),
        )
        for c in range(3):
            for a in range(4):
                first = field[c][:, 128 * a : 128 * a + 128]
                second = field[c][:, 128 * a + 512 : 128 * a + 640]
                even = jnp.where(half_row < 4, first, pltpu.roll(second, 4, 0))
                odd = jnp.where(half_row < 4, pltpu.roll(first, 4, 0), second)
                out_ref[2 * group, 4 * c + a] = even.astype(bf16)
                out_ref[2 * group + 1, 4 * c + a] = odd.astype(bf16)
        return carry

    lax.fori_loop(0, SLAB // 8, step, 0)


def electric(magnetic, velocity, low, high):
    return pl.pallas_call(
        electric_kernel,
        out_shape=jax.ShapeDtypeStruct((NT, 12, 8, 128), bf16),
        in_specs=[VMEM] * 4,
        out_specs=VMEM,
        scratch_shapes=[pltpu.VMEM((SLAB + 16, N), f32)] * 2,
        compiler_params=pltpu.CompilerParams(vmem_limit_bytes=24 << 20),
        cost_estimate=pl.CostEstimate(flops=8000000, bytes_accessed=4000000, transcendentals=0),
        name="electric",
    )(magnetic, velocity, low, high)


def small_tables(wave, quarter):
    def pair(rows, scale, back):
        phase = (np.arange(rows)[:, None] * scale * wave[None, :] - back[None, :]) % N
        angle = 2.0 * np.pi * phase / N
        return np.cos(angle).astype(np.float32), np.sin(angle).astype(np.float32)

    none = np.zeros_like(wave)
    return pair(8, 1, 256 * quarter) + pair(8, 8, none) + pair(16, 64, none)


def table_kernel(rc_ref, rs_ref, ic_ref, is_ref, mc_ref, ms_ref, *out_refs):
    m = pl.program_id(0)
    mc = mc_ref[pl.ds(m, 1), :]
    ms = ms_ref[pl.ds(m, 1), :]
    for lanes in range(0, rc_ref.shape[1], 512):
        cut = slice(lanes, lanes + 512)
        mid_c = ic_ref[:, cut] * mc[:, cut] - is_ref[:, cut] * ms[:, cut]
        mid_s = is_ref[:, cut] * mc[:, cut] + ic_ref[:, cut] * ms[:, cut]
        rc = rc_ref[:, cut]
        rs = rs_ref[:, cut]
        for i in range(0, 8, 2):
            cos_rows = []
            sin_rows = []
            for k in (i, i + 1):
                c = jnp.broadcast_to(mid_c[k : k + 1, :], rc.shape)
                s = jnp.broadcast_to(mid_s[k : k + 1, :], rc.shape)
                cos_rows.append(rc * c - rs * s)
                if len(out_refs) == 2:
                    sin_rows.append(-(rs * c) - rc * s)
            out_refs[0][8 * i : 8 * i + 16, cut] = jnp.concatenate(cos_rows, axis=0).astype(bf16)
            if len(out_refs) == 2:
                out_refs[1][8 * i : 8 * i + 16, cut] = jnp.concatenate(sin_rows, axis=0).astype(bf16)


def tables(small, count, name):
    width = small[0].shape[1]
    whole = lambda a: pl.BlockSpec(a.shape, lambda m: (0, 0))
    return pl.pallas_call(
        table_kernel,
        grid=(16,),
        out_shape=[jax.ShapeDtypeStruct((N, width), bf16)] * count,
        in_specs=[whole(a) for a in small],
        out_specs=[pl.BlockSpec((64, width), lambda m: (m, 0))] * count,
        cost_estimate=pl.CostEstimate(
            flops=12000000, bytes_accessed=count * N * width * 2, transcendentals=0
        ),
        name=name,
    )(*small)


def time_matrix():
    t = np.arange(NT)
    taper = 0.5 - 0.5 * np.cos(2.0 * np.pi * (t + 0.5) / NT)
    table = np.zeros((HALF, 2, NT))
    for f in range(HALF):
        angle = 2.0 * np.pi * ((f * t) % NT) / NT
        table[f, 0] = taper * np.cos(angle)
        table[f, 1] = -taper * np.sin(angle)
    table[0, 1] = taper * np.cos(2.0 * np.pi * ((HALF * t) % NT) / NT)
    spread = np.einsum("fpt,bd,ye->bfpytde", table, np.eye(2), np.eye(4))
    return spread.reshape(256, 256).astype(np.float32).astype(jnp.bfloat16)


def turn_kernel(field_ref, time_ref, table_ref, out_ref, left_ref):
    for c in range(3):
        cells = jnp.concatenate(
            [field_ref[:, 4 * c + a].reshape(NT * 8, 128) for a in range(4)], axis=1
        )
        timed = jnp.dot(time_ref[...], cells, preferred_element_type=f32).astype(bf16)
        left_ref[128 * c : 128 * c + 128, 0:512] = timed[0:128]
        left_ref[128 * c : 128 * c + 128, 512:1024] = timed[128:256]
    left = left_ref[...]
    row = lax.broadcasted_iota(jnp.int32, (8, 128), 0)
    for g in range(8):
        by_cos = jnp.dot(
            left, table_ref[:, 128 * g : 128 * g + 128], preferred_element_type=f32
        ).reshape(3, HALF, 8, 128)
        by_sin = jnp.dot(
            left, table_ref[:, N + 128 * g : N + 128 * g + 128], preferred_element_type=f32
        ).reshape(3, HALF, 8, 128)
        for c in range(3):
            for f in range(HALF):
                pc, ps = by_cos[c, f], by_sin[c, f]
                swapped = pltpu.roll(ps, 4, 0)
                if f == 0:
                    plus = jnp.where(row < 4, pc, -swapped)
                    minus = jnp.where(row < 4, pltpu.roll(pc, 4, 0), -ps)
                    low = 0
                else:
                    plus = jnp.where(row < 4, pc + swapped, pc - swapped)
                    minus = jnp.where(row < 4, pc - swapped, -pc - swapped)
                    low = HALF - f
                out_ref[(HALF + f) * 8 + g, c] = plus.astype(bf16)
                out_ref[low * 8 + g, c] = minus.astype(bf16)


def turn(field, time_table, table):
    return pl.pallas_call(
        turn_kernel,
        out_shape=jax.ShapeDtypeStruct((NT * 8, 3, 8, 128), bf16),
        in_specs=[VMEM] * 3,
        out_specs=VMEM,
        scratch_shapes=[pltpu.VMEM((384, N), bf16)],
        compiler_params=pltpu.CompilerParams(vmem_limit_bytes=32 << 20),
        cost_estimate=pl.CostEstimate(
            flops=2 * 384 * N * 2 * N, bytes_accessed=8000000, transcendentals=0
        ),
        name="turn",
    )(field, time_table, table)


ROWS = 256


def split_dot(exact, value, dims):
    high = value.astype(bf16)
    rest = (value - high.astype(f32)).astype(bf16)
    dot = lambda v: lax.dot_general(exact, v, dims, preferred_element_type=f32)
    return dot(high) + dot(rest)


def power_kernel(cells_ref, re_ref, im_ref, bins_ref, head_ref, power_ref, binned_ref, right_ref, sum_ref):
    step = pl.program_id(0)

    @pl.when(step == 0)
    def _():
        for c in range(3):
            right_ref[:, 128 * c : 128 * c + 128] = cells_ref[:, c].reshape(2 * N, 128)
        sum_ref[...] = jnp.zeros_like(sum_ref)

    wave_re = jnp.dot(re_ref[...], right_ref[...], preferred_element_type=f32)
    wave_im = jnp.dot(im_ref[...], right_ref[...], preferred_element_type=f32)
    square = wave_re * wave_re + wave_im * wave_im
    power = (square[:, 0:128] + square[:, 128:256] + square[:, 256:384]) * (1.0 / (NT * N * N))
    power_ref[0] = power
    lane = lax.broadcasted_iota(jnp.int32, (ROWS, BINS), 1)
    same_q = ((bins_ref[...] & (NBQ - 1)) == (lane & (NBQ - 1))).astype(f32).astype(bf16)
    sum_ref[...] += split_dot(same_q, power, (((0,), (0,)), ((), ())))

    @pl.when(step == N // ROWS - 1)
    def _():
        bin_row = lax.broadcasted_iota(jnp.int32, (BINS, SLAB), 0)
        by_bin = jnp.where(head_ref[...] // NBQ == bin_row // NBQ, sum_ref[...], 0.0)
        ones = jnp.ones((8, SLAB), bf16)
        binned_ref[...] = split_dot(ones, by_bin, (((1,), (1,)), ((), ())))[0:1]


def power_of(cells, re_table, im_table, mode_bin):
    return pl.pallas_call(
        power_kernel,
        grid=(N // ROWS,),
        out_shape=[
            jax.ShapeDtypeStruct((1, N, SLAB), f32),
            jax.ShapeDtypeStruct((1, BINS), f32),
        ],
        in_specs=[
            pl.BlockSpec((NT * 8, 3, 8, 128), lambda i: (0, 0, 0, 0)),
            pl.BlockSpec((ROWS, 2 * N), lambda i: (i, 0)),
            pl.BlockSpec((ROWS, 2 * N), lambda i: (i, 0)),
            pl.BlockSpec((ROWS, SLAB), lambda i: (i, 0)),
            pl.BlockSpec((BINS, SLAB), lambda i: (0, 0)),
        ],
        out_specs=[
            pl.BlockSpec((1, ROWS, SLAB), lambda i: (0, i, 0)),
            pl.BlockSpec((1, BINS), lambda i: (0, 0)),
        ],
        scratch_shapes=[pltpu.VMEM((2 * N, 384), bf16), pltpu.VMEM((BINS, SLAB), f32)],
        compiler_params=pltpu.CompilerParams(vmem_limit_bytes=32 << 20),
        cost_estimate=pl.CostEstimate(
            flops=2 * 2 * N * 2 * N * 384, bytes_accessed=12000000, transcendentals=0
        ),
        name="power",
    )(cells, re_table, im_table, mode_bin, mode_bin)


Z_SMALL = small_tables(np.arange(2 * N) % N, np.arange(2 * N) // N)


def y_columns():
    column = np.arange(2 * N)
    source = column // 8
    plane = SLAB * (source % 8) + 4 * (source // 8) + column % 4
    return plane, column // 4 % 2


Y_SMALL = small_tables(*y_columns())
TIME_TABLE = time_matrix()


def body(magnetic, velocity, mode_bin, omega_edges):
    ring = lax.axis_size("gy")
    first = jnp.stack([magnetic[0, 0, 1, 0], magnetic[0, 2, 1, 0]])
    last = jnp.stack([magnetic[0, 0, 1, SLAB - 1], magnetic[0, 2, 1, SLAB - 1]])
    low = lax.ppermute(last, "gy", [(i, (i + 1) % ring) for i in range(ring)])
    high = lax.ppermute(first, "gy", [((i + 1) % ring, i) for i in range(ring)])
    field = electric(magnetic, velocity, low, high)
    field = lax.all_to_all(field.reshape(NT, 96, 128), "tm", 0, 0, tiled=True)
    (z_table,) = tables([jnp.asarray(a) for a in Z_SMALL], 1, "z_table")
    turned = turn(field.reshape(NT, 12, 8, 128), jnp.asarray(TIME_TABLE), z_table)
    cells = lax.all_to_all(turned.reshape(NT * 8, 24, 128), ("tm", "gy"), 0, 0, tiled=True)
    re_table, im_table = tables([jnp.asarray(a) for a in Y_SMALL], 2, "y_table")
    power, by_mode = power_of(cells.reshape(NT * 8, 3, 8, 128), re_table, im_table, mode_bin)
    spread = jnp.broadcast_to(by_mode[None], (NT * 8, 1, BINS))
    every = lax.all_to_all(spread, ("tm", "gy"), 0, 0, tiled=True).reshape(NT, 8, BINS)
    omega = jnp.arange(NT, dtype=jnp.int32)
    member = (omega[None, :] >= omega_edges[:-1, None]) & (omega[None, :] < omega_edges[1:, None])
    binned = jnp.sum(jnp.where(member[:, :, None, None], every[None], 0.0), axis=(1, 2))
    spectrum = jnp.log(binned * (NB_W * BINS) / (NT * N * N) + 1e-06)
    return power, spectrum


def solution(mesh):
    return jax.shard_map(
        body,
        mesh=mesh,
        in_specs=(
            P("tm", None, None, "gy", None),
            P("tm", None, None, "gy", None),
            P(None, "gy"),
            P(),
        ),
        out_specs=(P("tm", None, "gy"), P()),
        check_vma=False,
    )
```

time: 518 us -> 141 us (0.27)
  matrix products: 215 us -> 0 us
  waiting for transfers between devices: 169 us -> 64.3 us
  blocking collectives: 75.6 us -> 0 us
  Pallas kernels: 0 us -> 31.7 us
  starting transfers between devices: 12.7 us -> 31.5 us
  between operations: 14.5 us -> 0.71 us
  local copies, waits for them, and re-layouts: 19.7 us -> 11 us
    dot_general x26 -> x0, matrix products: 215 us -> none  [the longest x16 28.7 us: add_block(): return summed + jnp.dot(row_block, onehot, precision=highest)]
    all_gather x1 -> x0, waiting for transfers between devices: 142 us -> none  [body(): time_segment = lax.all_gather(electric, 'tm', axis=0, tiled=True)]
    psum x1 -> x0, blocking collectives: 75.6 us -> none  [body(): binned = lax.psum(partial_value, ('tm', 'gy'))]
    all_to_all x1 -> x3, waiting for transfers between devices: 22.9 us -> 58.3 us  [the longest x1 32.3 us: body(): lax.all_to_all(turned.reshape(NT * 8, 24, 128), ('tm', 'gy'), 0, 0, tiled...]
    pallas_call x0 -> x5, Pallas kernels: none -> 31.7 us  [the longest x2 17.1 us: tables(): pl.pallas_call(table_kernel, grid=(16,), out_shape=[jax.ShapeDtypeStruct(...]
    all_to_all x1 -> x3, starting transfers between devices: 6.66 us -> 25.4 us  [the longest x1 10.8 us: body(): field = lax.all_to_all(field.reshape(NT, 96, 128), 'tm', 0, 0, tiled=True)]
    eq x16 -> x0, local copies, waits for them, and re-layouts: 12.3 us -> none  [add_block(): onehot = (bin_ids[:, None] == bin_range[None, :]).astype(jnp.float32)]
    unnamed x8 -> x16, local copies, waits for them, and re-layouts: 0.02 us -> 9.38 us
  transfers between devices with their start and end apart: 4 -> 5, of which waited for: 3 -> 5; matrix products, arithmetic and copies ran while one was open for 0% -> 0% of each run, Pallas kernels for 0% -> 12%
where the time goes in v1:
time: 141 us; the launch traced here: 140 us
  waiting for transfers between devices  64.3 us (46%)
  Pallas kernels  31.7 us (22%)
  starting transfers between devices  31.5 us (22%)
  local copies, waits for them, and re-layouts  11 us (8%)
    all_to_all x1, waiting for transfers between devices, body(): lax.all_to_all(turned.reshape(NT * 8, 24, 128), ('tm', 'gy'), 0, 0, tiled...  32.3 us
    pallas_call x2, Pallas kernels, tables(): pl.pallas_call(table_kernel, grid=(16,), out_shape=[jax.ShapeDtypeStruct(...  17.1 us
    all_to_all x1, waiting for transfers between devices, body(): field = lax.all_to_all(field.reshape(NT, 96, 128), 'tm', 0, 0, tiled=True)  13.3 us
    all_to_all x1, waiting for transfers between devices, body(): lax.all_to_all(spread, ('tm', 'gy'), 0, 0, tiled=True).reshape(NT, 8, BINS)  12.6 us
    all_to_all x1, starting transfers between devices, body(): field = lax.all_to_all(field.reshape(NT, 96, 128), 'tm', 0, 0, tiled=True)  10.8 us
    unnamed x16, local copies, waits for them, and re-layouts  9.38 us
    all_to_all x1, starting transfers between devices, body(): lax.all_to_all(turned.reshape(NT * 8, 24, 128), ('tm', 'gy'), 0, 0, tiled...  7.49 us
    all_to_all x1, starting transfers between devices, body(): lax.all_to_all(spread, ('tm', 'gy'), 0, 0, tiled=True).reshape(NT, 8, BINS)  7.08 us
  transfers between devices with their start and end apart: 5, of which 5 were waited for; matrix products, arithmetic and copies ran while one was open for 0% of the time, Pallas kernels for 12%

profile of v1, /device:TPU:1, one launch (start us, length us, event | category | flops | bytes accessed | tf_op | source)
XLA Modules:
  0.0 140.3 jit_solution(13142163968744800588)
XLA Ops:
  0.6 0.8 slice_bitcast_fusion.1
  1.4 6.0 %collective-permute-start.1 = (bf16[2,1024]{1,0:T(2,128)(2,1)S(1)}, bf16[2,1024]{1,0:T(2,128)(2,1)S(1)}, u32[]{:S(2)}, u32[]{:S(2)}) collective-permute-start(bf16[2,1024]{1,0:T(2,128)(2,1)S(1)} %pad_maximum_fusion.1), channel_id=1, source_target_pairs={{1,0},{2,1},{3,2},{4,3},{5,4},{6,5},{7,6},{0,7},{9,8},{10,9},{11,1... | collective-permute-start | bytes 12296 | tf_op jit(solution)/shard_map/ppermute | solution.py:292
  7.5 0.1 collective-permute-start
  7.6 0.6 collective-permute-done.1.high_ref
  8.2 5.4 %collective-permute-done.low_ref = bf16[2,1024]{1,0:T(2,128)(2,1)S(1)} collective-permute-done((bf16[2,1024]{1,0:T(2,128)(2,1)S(1)}, bf16[2,1024]{1,0:T(2,128)(2,1)S(1)}, u32[]{:S(2)}, u32[]{:S(2)}) %collective-permute-start) | collective-permute-done | bytes 4128 | tf_op jit(solution)/shard_map/ppermute | solution.py:291
  13.6 0.0 copy-start.1
  13.6 1.7 %copy-done.1 = bf16[1,3,3,128,1024]{4,3,2,1,0:T(8,128)(2,1)S(1)} copy-done((bf16[1,3,3,128,1024]{4,3,2,1,0:T(8,128)(2,1)S(1)}, bf16[1,3,3,128,1024]{4,3,2,1,0:T(8,128)(2,1)}, u32[]{:S(2)}) %copy-start.1) | copy-done | bytes 2359320
  15.3 0.0 copy-start.2
  15.3 1.1 copy-done.2
  16.4 2.8 %electric.1 = bf16[32,12,8,128]{3,2,1,0:T(8,128)(2,1)} custom-call(bf16[1,3,3,128,1024]{4,3,2,1,0:T(8,128)(2,1)S(1)} %copy-done.1, bf16[1,3,1,128,1024]{4,3,2,1,0:T(8,128)(2,1)S(1)} %copy-done.2, bf16[2,1024]{1,0:T(2,128)(2,1)S(1)} %collective-permute-done.low_ref, bf16[2,1024]{1,0:T(2,128)(2,1)S(1)} %collective-permute-done.1.high_ref), custom_call_target="tpu_custom_call" | custom-call | flops 8000000 | bytes 4000000 | tf_op jit(solution)/shard_map/electric/pallas_call | solution.py:86
  19.3 10.8 %all-to-all-start = ((bf16[32,96,128]{2,1,0:T(8,128)(2,1)}), bf16[32,96,128]{2,1,0:T(8,128)(2,1)S(1)}, u32[]{:S(2)}, u32[]{:S(2)}) async-start(bf16[32,96,128]{2,1,0:T(8,128)(2,1)} %bitcast.4), calls=%async_computation | async-start | bytes 1572864 | tf_op jit(solution)/shard_map/all_to_all | solution.py:294
  30.1 0.0 copy-start.3
  30.1 7.9 %z_table.1.table_ref = bf16[1024,2048]{1,0:T(8,128)(2,1)} custom-call(f32[8,2048]{1,0:T(8,128)} %constant.35.clone.rc_ref, f32[8,2048]{1,0:T(8,128)} %constant.36.clone.rs_ref, f32[8,2048]{1,0:T(8,128)} %constant.37.clone.ic_ref, f32[8,2048]{1,0:T(8,128)} %constant.38.clone.is_ref, f32[16,2048]{1,0:T(8,128)} %constant.39.clone.mc_ref, ...), custom_call_target="tpu_custom_call" | custom-call | flops 12000000 | bytes 4194304 | tf_op jit(solution)/shard_map/z_table/pallas_call | solution.py:135
  38.0 13.3 %all-to-all-done = bf16[32,96,128]{2,1,0:T(8,128)(2,1)S(1)} async-done(((bf16[32,96,128]{2,1,0:T(8,128)(2,1)}), bf16[32,96,128]{2,1,0:T(8,128)(2,1)S(1)}, u32[]{:S(2)}, u32[]{:S(2)}) %all-to-all-start) | async-done | bytes 786464 | tf_op jit(solution)/shard_map/all_to_all | solution.py:294
  51.4 0.0 copy-done.3
  51.4 2.2 %copy-done = bf16[1024,2048]{1,0:T(8,128)(2,1)S(1)} copy-done((bf16[1024,2048]{1,0:T(8,128)(2,1)S(1)}, bf16[1024,2048]{1,0:T(8,128)(2,1)}, u32[]{:S(2)}) %copy-start) | copy-done | bytes 4194328
  53.5 4.8 %turn.1 = bf16[256,3,8,128]{3,2,1,0:T(8,128)(2,1)} custom-call(bf16[32,12,8,128]{3,2,1,0:T(8,128)(2,1)S(1)} %bitcast.14, bf16[256,256]{1,0:T(8,128)(2,1)S(1)} %copy-done.3, bf16[1024,2048]{1,0:T(8,128)(2,1)S(1)} %copy-done), custom_call_target="tpu_custom_call" | custom-call | flops 1610612736 | bytes 8000000 | tf_op jit(solution)/shard_map/turn/pallas_call | solution.py:195
  58.4 7.5 %all-to-all-start.1 = ((bf16[256,24,128]{2,1,0:T(8,128)(2,1)}), bf16[256,24,128]{2,1,0:T(8,128)(2,1)S(1)}, u32[]{:S(2)}, u32[]{:S(2)}) async-start(bf16[256,24,128]{2,1,0:T(8,128)(2,1)} %bitcast.6), calls=%async_computation.1 | async-start | bytes 3145728 | tf_op jit(solution)/shard_map/all_to_all | solution.py:297
  65.9 9.2 %y_table.1 = (bf16[1024,2048]{1,0:T(8,128)(2,1)}, bf16[1024,2048]{1,0:T(8,128)(2,1)}) custom-call(f32[8,2048]{1,0:T(8,128)} %constant.42.clone.rc_ref, f32[8,2048]{1,0:T(8,128)} %constant.43.clone.rs_ref, f32[8,2048]{1,0:T(8,128)} %constant.44.clone.ic_ref, f32[8,2048]{1,0:T(8,128)} %constant.45.clone.is_ref, f32[16,2048]{1,0:T(8,128)} %constant.46.clone.mc_ref, ...), custom_call_target="tpu_custom_call" | custom-call | flops 12000000 | bytes 8388608 | tf_op jit(solution)/shard_map/y_table/pallas_call | solution.py:135
  75.1 32.3 %all-to-all-done.1 = bf16[256,24,128]{2,1,0:T(8,128)(2,1)S(1)} async-done(((bf16[256,24,128]{2,1,0:T(8,128)(2,1)}), bf16[256,24,128]{2,1,0:T(8,128)(2,1)S(1)}, u32[]{:S(2)}, u32[]{:S(2)}) %all-to-all-start.1) | async-done | bytes 1572896 | tf_op jit(solution)/shard_map/all_to_all | solution.py:297
  107.5 0.0 copy-done.6
  107.5 2.2 %copy-done.4 = bf16[1024,2048]{1,0:T(8,128)(2,1)S(1)} copy-done((bf16[1024,2048]{1,0:T(8,128)(2,1)S(1)}, bf16[1024,2048]{1,0:T(8,128)(2,1)}, u32[]{:S(2)}) %copy-start.4) | copy-done | bytes 4194328
  109.6 2.2 %copy-done.5 = bf16[1024,2048]{1,0:T(8,128)(2,1)S(1)} copy-done((bf16[1024,2048]{1,0:T(8,128)(2,1)S(1)}, bf16[1024,2048]{1,0:T(8,128)(2,1)}, u32[]{:S(2)}) %copy-start.5) | copy-done | bytes 4194328
  111.8 6.9 %power.1 = (f32[1,1024,128]{2,1,0:T(8,128)}, f32[1,128]{1,0:T(1,128)S(1)}) custom-call(bf16[256,3,8,128]{3,2,1,0:T(8,128)(2,1)S(1)} %bitcast.15, bf16[1024,2048]{1,0:T(8,128)(2,1)S(1)} %copy-done.4, bf16[1024,2048]{1,0:T(8,128)(2,1)S(1)} %copy-done.5, s32[1024,128]{1,0:T(8,128)S(1)} %copy-done.6, s32[1024,128]{1,0:T(8,128)S(1)} %copy-done.6), custom_call_target="tpu_custom_call" | custom-call | flops 3221225472 | bytes 12000000 | tf_op jit(solution)/shard_map/power/pallas_call | solution.py:246
  118.7 0.7 broadcast_in_dim.37
  119.4 7.1 %all-to-all-start.2 = ((f32[256,1,128]{2,1,0:T(1,128)}), f32[256,1,128]{2,1,0:T(1,128)S(1)}, u32[]{:S(2)}, u32[]{:S(2)}) async-start(f32[256,1,128]{2,1,0:T(1,128)} %broadcast_in_dim.37), calls=%async_computation.2 | async-start | bytes 262144 | tf_op jit(solution)/shard_map/all_to_all | solution.py:301
  126.5 0.0 copy-done.7
  126.5 0.1 fusion.1
  126.6 0.1 fusion
  126.7 12.6 %all-to-all-done.2 = f32[256,1,128]{2,1,0:T(1,128)S(1)} async-done(((f32[256,1,128]{2,1,0:T(1,128)}), f32[256,1,128]{2,1,0:T(1,128)S(1)}, u32[]{:S(2)}, u32[]{:S(2)}) %all-to-all-start.2) | async-done | bytes 131104 | tf_op jit(solution)/shard_map/all_to_all | solution.py:301
  139.3 0.3 select_reduce_fusion
  139.6 0.6 add_log_fusion
  (7 shorter events, 0.0 us)
Async XLA Ops:
  1.4 6.8 %collective-permute-start.1 = (bf16[2,1024]{1,0:T(2,128)(2,1)S(1)}, bf16[2,1024]{1,0:T(2,128)(2,1)S(1)}, u32[]{:S(2)}, u32[]{:S(2)}) collective-permute-start(bf16[2,1024]{1,0:T(2,128)(2,1)S(1)} %pad_maximum_fusion.1), channel_id=1, source_target_pairs={{1,0},{2,1},{3,2},{4,3},{5,4},{6,5},{7,6},{0,7},{9,8},{10,9},{11,1... | collective-permute-start | bytes 12296 | tf_op jit(solution)/shard_map/ppermute | solution.py:292
  7.5 6.1 %collective-permute-start = (bf16[2,1024]{1,0:T(2,128)(2,1)S(1)}, bf16[2,1024]{1,0:T(2,128)(2,1)S(1)}, u32[]{:S(2)}, u32[]{:S(2)}) collective-permute-start(bf16[2,1024]{1,0:T(2,128)(2,1)S(1)} %pad_maximum_fusion), channel_id=1, source_target_pairs={{0,1},{1,2},{2,3},{3,4},{4,5},{5,6},{6,7},{7,0},{8,9},{9,10},{10,1... | collective-permute-start | bytes 12296 | tf_op jit(solution)/shard_map/ppermute | solution.py:291
  13.6 1.7 %copy-start.1 = (bf16[1,3,3,128,1024]{4,3,2,1,0:T(8,128)(2,1)S(1)}, bf16[1,3,3,128,1024]{4,3,2,1,0:T(8,128)(2,1)}, u32[]{:S(2)}) copy-start(bf16[1,3,3,128,1024]{4,3,2,1,0:T(8,128)(2,1)} %mag_ref.1) | copy-start | bytes 7077892
  15.3 1.1 copy-start.2
  19.3 32.1 %all-to-all-start = ((bf16[32,96,128]{2,1,0:T(8,128)(2,1)}), bf16[32,96,128]{2,1,0:T(8,128)(2,1)S(1)}, u32[]{:S(2)}, u32[]{:S(2)}) async-start(bf16[32,96,128]{2,1,0:T(8,128)(2,1)} %bitcast.4), calls=%async_computation | async-start | bytes 1572864 | tf_op jit(solution)/shard_map/all_to_all | solution.py:294
  30.1 21.2 %copy-start.3 = (bf16[256,256]{1,0:T(8,128)(2,1)S(1)}, bf16[256,256]{1,0:T(8,128)(2,1)}, u32[]{:S(2)}) copy-start(bf16[256,256]{1,0:T(8,128)(2,1)} %constant.41.clone.time_ref) | copy-start | bytes 393220
  51.4 2.2 %copy-start = (bf16[1024,2048]{1,0:T(8,128)(2,1)S(1)}, bf16[1024,2048]{1,0:T(8,128)(2,1)}, u32[]{:S(2)}) copy-start(bf16[1024,2048]{1,0:T(8,128)(2,1)} %z_table.1.table_ref) | copy-start | bytes 12582916
  58.4 49.1 %copy-start.6 = (s32[1024,128]{1,0:T(8,128)S(1)}, s32[1024,128]{1,0:T(8,128)}, u32[]{:S(2)}) copy-start(s32[1024,128]{1,0:T(8,128)} %head_ref.1) | copy-start | bytes 1572868
  58.4 49.1 %all-to-all-start.1 = ((bf16[256,24,128]{2,1,0:T(8,128)(2,1)}), bf16[256,24,128]{2,1,0:T(8,128)(2,1)S(1)}, u32[]{:S(2)}, u32[]{:S(2)}) async-start(bf16[256,24,128]{2,1,0:T(8,128)(2,1)} %bitcast.6), calls=%async_computation.1 | async-start | bytes 3145728 | tf_op jit(solution)/shard_map/all_to_all | solution.py:297
  107.5 2.2 %copy-start.4 = (bf16[1024,2048]{1,0:T(8,128)(2,1)S(1)}, bf16[1024,2048]{1,0:T(8,128)(2,1)}, u32[]{:S(2)}) copy-start(bf16[1024,2048]{1,0:T(8,128)(2,1)} %get-tuple-element.6.re_ref) | copy-start | bytes 12582916
  109.6 2.2 %copy-start.5 = (bf16[1024,2048]{1,0:T(8,128)(2,1)S(1)}, bf16[1024,2048]{1,0:T(8,128)(2,1)}, u32[]{:S(2)}) copy-start(bf16[1024,2048]{1,0:T(8,128)(2,1)} %get-tuple-element.7.im_ref) | copy-start | bytes 12582916
  111.8 14.7 %copy-start.7 = (s32[9]{0:T(128)S(1)}, s32[9]{0:T(128)}, u32[]{:S(2)}) copy-start(s32[9]{0:T(128)} %param.20) | copy-start | bytes 112
  119.4 19.9 %all-to-all-start.2 = ((f32[256,1,128]{2,1,0:T(1,128)}), f32[256,1,128]{2,1,0:T(1,128)S(1)}, u32[]{:S(2)}, u32[]{:S(2)}) async-start(f32[256,1,128]{2,1,0:T(1,128)} %broadcast_in_dim.37), calls=%async_computation.2 | async-start | bytes 262144 | tf_op jit(solution)/shard_map/all_to_all | solution.py:301
